TPU v7x, 32 devices: a whole 2x2x4 slice. The times are simulated.
32 devices in a mesh: grp: 2 (over y), tok: 16 (over z, x, core).
Axes of the slice: x: 2, y: 2, z: 4, core: 2. Of those that a mesh axis runs over, the one named last changes fastest.
Arguments:
- hidden: bfloat16 [4, 1024, 1536], P('grp', 'tok'), parts along dimension 0
- base_ids: int32 [4, 1024], P('grp', 'tok'), parts along dimension 0, may hold values from 0 to 4, as said below
- attn_gain: bfloat16 [1536], replicated, may hold values from 0.099609375 to 1.8984375
- q_weight: bfloat16 [1536, 768], replicated
- kv_weight: bfloat16 [1536, 384], replicated
- out_weight: bfloat16 [768, 1536], replicated, may hold values from -0.21875 to 0.21875
- head_gain: bfloat16 [1536], replicated, may hold values from 0.099609375 to 1.8984375
- head_weight: bfloat16 [1536, 1536], replicated, may hold values from -0.15625 to 0.15625
- head_bias: float32 [1536], replicated, may hold values from -1 to 1
- track_perm: int32 [1536], replicated, may hold values from 0 to 1535, each once
Outputs:
- combined: float32 [2048, 1536], P(('grp', 'tok')), parts along dimension 0
There are 2 independent parts, one for each index of `grp`. A program takes and returns all parts, laid end to end along the dimension named above; an argument that names none is the same for every part. Nothing has to cross between parts.
Inputs may be any that keep to these rules, and one draw needn't show every extreme that they name: `base_ids`: every eighth token of each strand, from token 0, has a base 0 to 3.
All inputs are finite; a program needn't handle non-finite values.
Results may differ from a plain program's by a relative error of at most 0.0058.
Values may be sent and summed in bfloat16 or wider, within the bound.
No kernel may reach another device: no remote copies, remote signals or barrier semaphores. Data moves between devices by JAX's collectives and lax.ppermute only.
A program may use at most 128 MiB of HBM per device.

v0:
```python
import math
import jax
import jax.numpy as jnp
from jax import lax
from jax.sharding import PartitionSpec as P


def swapped(value, axis, distance):
    mask = 2**distance
    pairs = [(source, source ^ mask) for source in range(lax.axis_size(axis))]
    return lax.ppermute(value, axis, pairs)


def normalize(rows, gain):
    widened = rows.astype(jnp.float32)
    return (
        widened
        * lax.rsqrt(jnp.mean(widened * widened, -1, keepdims=True) + 1e-06)
        * gain.astype(jnp.float32)
    )


def attend(running, queries, key_value, usable_flag):
    maxima, totals, accumulated = running
    width_head = queries.shape[2]
    key_rows = key_value[:, :, :width_head]
    value_rows = key_value[:, :, width_head:]
    scores = jnp.einsum("srd,skd->srk", queries, key_rows, preferred_element_type=jnp.float32) * (
        1.0 / math.sqrt(width_head)
    )
    usable = usable_flag[:, None, :] > 0
    scores = jnp.where(usable, scores, jnp.float32(-1e30))
    new_maxima = jnp.maximum(maxima, jnp.max(scores, -1))
    weight_exp = jnp.where(usable, jnp.exp(scores - new_maxima[:, :, None]), jnp.float32(0.0))
    totals = jnp.sum(weight_exp, -1)
    summed = jnp.einsum(
        "srk,skd->srd",
        weight_exp.astype(jnp.bfloat16),
        value_rows,
        preferred_element_type=jnp.float32,
    )
    accumulated = summed
    return (new_maxima, totals, accumulated)


def per_device(
    hidden,
    base_ids,
    attn_gain,
    q_weight,
    kv_weight,
    out_weight,
    head_gain,
    head_weight,
    head_bias,
    track_perm,
):
    tok_rows = hidden.shape[1]
    width_head = kv_weight.shape[1] // 2
    head_count = q_weight.shape[1] // width_head
    bit_count = lax.axis_size("tok").bit_length() - 1
    normed = normalize(hidden, attn_gain).astype(jnp.bfloat16)
    key_value = jnp.einsum(
        "std,de->ste", normed, kv_weight, preferred_element_type=jnp.float32
    ).astype(jnp.bfloat16)
    usable_flag = (base_ids != 4).astype(jnp.bfloat16)
    partner = hidden[1]
    for bit_number in range(bit_count):
        partner = swapped(partner, "tok", bit_number)
    partner = partner[::-1]
    query_source = jnp.stack([normed[0], normalize(partner, attn_gain).astype(jnp.bfloat16)])
    residual_base = jnp.stack([hidden[0], partner])
    queries = jnp.einsum(
        "std,de->ste", query_source, q_weight, preferred_element_type=jnp.float32
    ).astype(jnp.bfloat16)
    queries = queries.reshape(2, tok_rows * head_count, width_head)
    row_count = queries.shape[1]
    start_state = (
        jnp.full((2, row_count), -1e30, jnp.float32),
        jnp.zeros((2, row_count), jnp.float32),
        jnp.zeros((2, row_count, width_head), jnp.float32),
    )
    softmax_state = attend(
        start_state,
        queries,
        lax.all_gather(key_value, "tok", axis=1, tiled=True),
        lax.all_gather(usable_flag, "tok", axis=1, tiled=True),
    )
    maxima, totals, accumulated = softmax_state
    attended = (
        (accumulated / totals[:, :, None])
        .astype(jnp.bfloat16)
        .reshape(2, tok_rows, head_count * width_head)
    )
    residual_sum = residual_base.astype(jnp.float32) + jnp.einsum(
        "ste,ed->std", attended, out_weight, preferred_element_type=jnp.float32
    )
    normed_out = normalize(residual_sum, head_gain).astype(jnp.bfloat16)
    forward_logits = (
        jnp.dot(normed_out[0], head_weight, preferred_element_type=jnp.float32) + head_bias
    )
    reverse_logits = (
        jnp.dot(normed_out[1], head_weight[:, track_perm], preferred_element_type=jnp.float32)
        + head_bias[track_perm]
    )
    forward_pred = jax.nn.softplus(forward_logits).astype(jnp.bfloat16)
    reverse_pred = jax.nn.softplus(reverse_logits).astype(jnp.bfloat16)
    return 0.5 * (forward_pred.astype(jnp.float32) + reverse_pred.astype(jnp.float32))


def solution(mesh):
    placed = (P("grp", "tok", None), P("grp", "tok"), P(), P(), P(), P(), P(), P(), P(), P())
    return jax.shard_map(
        per_device, mesh=mesh, in_specs=placed, out_specs=P(("grp", "tok"), None), check_vma=False
    )
```

profile of v0, /device:TPU:0, one launch (start us, length us, event | category | flops | bytes accessed | tf_op | source)
XLA Modules:
  0.0 101.3 jit_solution(12420879725566651075)
XLA Ops:
  6.5 0.0 copy-start
  6.5 0.0 copy-start.2
  6.5 0.0 copy-start.7
  6.5 0.0 all-gather.3.cloned.1.call-start
  6.6 0.8 convert_element_type.55
  7.4 1.2 %fusion.25 = f32[2,64]{1,0:T(2,128)S(1)} fusion(bf16[2,64,1536]{2,1,0:T(8,128)(2,1)} %param.10), kind=kLoop, calls=%fused_computation.31 | loop fusion | flops 589696 | bytes 393728 | tf_op jit(solution)/shard_map/reduce_sum | solution.py:18
  8.6 1.2 %fusion.27 = bf16[2,64,1536]{2,1,0:T(8,128)(2,1)S(1)} fusion(bf16[2,64,1536]{2,1,0:T(8,128)(2,1)} %param.10, f32[1536]{0:T(1024)S(1)} %convert_element_type.55, f32[2,64]{1,0:T(2,128)S(1)} %add_rsqrt_fusion.1), kind=kLoop, calls=%fused_computation.33 | loop fusion | flops 786432 | bytes 793088 | tf_op jit(solution)/shard_map/convert_element_type | solution.py:62
  9.8 0.0 copy-start.3
  9.8 2.4 %fusion.13 = bf16[2,64,384]{2,1,0:T(8,128)(2,1)} fusion(bf16[2,64,1536]{2,1,0:T(8,128)(2,1)S(1)} %fusion.27, bf16[1536,384]{1,0:T(8,128)(2,1)} %param.14), kind=kOutput, calls=%fused_computation.20 | convolution fusion | flops 151044096 | bytes 1671168 | tf_op jit(solution)/shard_map/std,de->ste/dot_general | solution.py:63
  12.2 0.0 all-gather.3.cloned.1.call-update
  12.2 0.0 copy-done.2
  12.3 0.6 collective-permute-start
  12.8 1.1 %collective-permute-done = bf16[64,1536]{1,0:T(8,128)(2,1)S(1)} collective-permute-done((bf16[64,1536]{1,0:T(8,128)(2,1)S(1)}, bf16[64,1536]{1,0:T(8,128)(2,1)S(1)}, u32[]{:S(2)}, u32[]{:S(2)}) %collective-permute-start) | collective-permute-done | bytes 196640 | tf_op jit(solution)/shard_map/ppermute | solution.py:11
  13.9 2.8 %collective-permute-start.1 = (bf16[64,1536]{1,0:T(8,128)(2,1)S(1)}, bf16[64,1536]{1,0:T(8,128)(2,1)S(1)}, u32[]{:S(2)}, u32[]{:S(2)}) collective-permute-start(bf16[64,1536]{1,0:T(8,128)(2,1)S(1)} %collective-permute-done), channel_id=1, source_target_pairs={{0,2},{1,3},{2,0},{3,1},{4,6},{5,7},{6,4},{7,5},{8,10},{9,11},{10,... | collective-permute-start | bytes 589832 | tf_op jit(solution)/shard_map/ppermute | solution.py:11
  16.7 0.0 copy-done.7
  16.7 20.7 %all-gather = bf16[16,64,2]{1,2,0:T(2,128)(2,1)S(1)} all-gather(bf16[1,64,2]{1,2,0:T(2,128)(2,1)S(1)} %fusion.37), channel_id=1, replica_groups=mesh['grp'=2,'tok'=16] {'tok'}, dimensions={0}, use_global_device_ids=true | all-gather | bytes 4352 | tf_op jit(solution)/shard_map/all_gather | solution.py:87
  37.4 0.0 collective-permute-done.1
  37.4 0.0 collective-permute-start.2
  37.4 0.0 copy-done.4
  37.4 11.5 %collective-permute-done.2 = bf16[64,1536]{1,0:T(8,128)(2,1)} collective-permute-done((bf16[64,1536]{1,0:T(8,128)(2,1)S(1)}, bf16[64,1536]{1,0:T(8,128)(2,1)}, u32[]{:S(2)}, u32[]{:S(2)}) %collective-permute-start.2) | collective-permute-done | bytes 196640 | tf_op jit(solution)/shard_map/ppermute | solution.py:11
  48.9 0.0 collective-permute-start.3
  48.9 0.0 copy-start.5
  48.9 6.7 %copy.26 = bf16[1536,1536]{0,1:T(8,128)(2,1)} copy(bf16[1536,1536]{1,0:T(8,128)(2,1)} %param.17) | data formatting | bytes 9437184 | tf_op args[7]
  55.6 0.0 copy-done.3
  55.7 0.1 reshape.64
  55.7 0.0 copy-done.5
  55.8 0.0 copy-start.1
  55.8 13.4 %gather_fusion = bf16[1536,1536]{1,0:T(8,128)(2,1)} fusion(bf16[1536,1536]{0,1:T(8,128)(2,1)} %copy.26, s32[2048]{0:T(1024)S(1)} %pad_clamp_fusion), kind=kCustom, calls=%fused_computation | custom fusion | bytes 9443328 | tf_op jit(solution)/shard_map/gather | solution.py:103
  69.2 0.0 copy-done.1
  69.2 8.4 %gather_fusion.1 = f32[1536]{0:T(1024)S(1)} fusion(f32[1536]{0:T(1024)S(1)} %copy-done.1, s32[2048]{0:T(1024)S(1)} %pad_clamp_fusion), kind=kCustom, calls=%fused_computation.1 | custom fusion | bytes 18432 | tf_op jit(solution)/shard_map/gather | solution.py:104
  77.5 0.0 collective-permute-done.3
  77.6 0.3 rev.3
  77.9 0.1 fusion.28
  78.1 0.1 fusion.36
  78.2 0.0 slice-done
  78.2 2.2 %fusion.10 = bf16[2,64,768]{2,1,0:T(8,128)(2,1)S(1)} fusion(bf16[1536,768]{1,0:T(8,128)(2,1)} %param.13, bf16[1,64,1536]{2,1,0:T(8,128)(2,1)S(1)} %fusion.36, bf16[1,64,1536]{2,1,0:T(8,128)(2,1)S(1)} %slice-done), kind=kOutput, calls=%fused_computation.19 | convolution fusion | flops 302284800 | bytes 2949120 | tf_op jit(solution)/shard_map/std,de->ste/dot_general | solution.py:73
  80.4 1.0 reshape.41
  81.3 2.0 %fusion.4 = (f32[2,256]{1,0:T(2,128)S(1)}, f32[2,256,1024]{2,1,0:T(8,128)S(1)}) fusion(pred[2,1024]{1,0:T(4,128)(4,1)S(1)} %bitcast.40, bf16[2,256,192]{2,1,0:T(8,128)(2,1)} %reshape.41, bf16[2,1024,384]{2,1,0:T(8,128)(2,1)} %all-gather.3.cloned.1.call-done), kind=kOutput, calls=%fused_computation.10 | convolution fusion | flops 202898944 | bytes 3411968 | tf_op jit(solution)/shard_map/srd,skd->srk/dot_general | solution.py:28
  83.4 0.6 fusion.5
  84.0 0.0 copy-done.6
  84.0 1.2 %fusion.9 = bf16[2,256,192]{1,2,0:T(8,128)(2,1)S(1)} fusion(f32[2,256,1024]{2,1,0:T(8,128)S(1)} %get-tuple-element.8, bf16[2,1024,384]{2,1,0:T(8,128)(2,1)S(1)} %copy-done.6, f32[2,256]{1,0:T(2,128)S(1)} %broadcast_maximum_fusion, pred[2,1024]{1,0:T(4,128)(4,1)S(1)} %bitcast.42, f32[2,256]{1,0:T(2,128)S(1)} %fusion.5), kind=kOutput, calls=%fused_computation.18 | convolution fusion | flops 204144640 | bytes 3350528 | tf_op jit(solution)/shard_map/srk,skd->srd/dot_general | solution.py:36
  85.2 0.1 copy.25
  85.3 0.3 reshape.42
  85.6 0.0 copy-done
  85.6 0.6 multiply_reduce_fusion
  86.2 0.2 multiply_convert_fusion
  86.4 3.4 %fusion.31 = bf16[64,1536]{1,0:T(8,128)(2,1)S(1)} fusion(bf16[1536,1536]{1,0:T(8,128)(2,1)} %param.17, bf16[2,64,1536]{2,1,0:T(8,128)(2,1)S(1)} %multiply_convert_fusion, f32[1536]{0:T(1024)S(1)} %copy-done.1), kind=kOutput, calls=%fused_computation.42 | convolution fusion | flops 302776320 | bytes 5120000 | tf_op jit(solution)/shard_map/dot_general | solution.py:100
  89.8 4.7 %add_multiply_fusion = f32[64,1536]{1,0:T(8,128)} fusion(bf16[1536,1536]{1,0:T(8,128)(2,1)} %gather_fusion, bf16[64,1536]{1,0:T(8,128)(2,1)S(1)} %fusion.31, bf16[2,64,1536]{2,1,0:T(8,128)(2,1)S(1)} %multiply_convert_fusion, f32[1536]{0:T(1024)S(1)} %gather_fusion.1), kind=kOutput, calls=%fused_computation.48 | convolution fusion | flops 303169536 | bytes 5513216 | tf_op jit(solution)/shard_map/dot_general | solution.py:103
  (15 shorter events, 0.1 us)
Async XLA Ops:
  6.5 79.1 %copy-start = (bf16[768,1536]{1,0:T(8,128)(2,1)S(1)}, bf16[768,1536]{1,0:T(8,128)(2,1)}, u32[]{:S(2)}) copy-start(bf16[768,1536]{1,0:T(8,128)(2,1)} %param.15) | copy-start | bytes 7077892
  6.5 5.7 %copy-start.2 = (bf16[2,64,1536]{2,1,0:T(8,128)(2,1)S(1)}, bf16[2,64,1536]{2,1,0:T(8,128)(2,1)}, u32[]{:S(2)}) copy-start(bf16[2,64,1536]{2,1,0:T(8,128)(2,1)} %param.10) | copy-start | bytes 1179652
  6.5 10.2 %copy-start.7 = (s32[2,64]{1,0:T(2,128)S(1)}, s32[2,64]{1,0:T(2,128)}, u32[]{:S(2)}) copy-start(s32[2,64]{1,0:T(2,128)} %param.11) | copy-start | bytes 1540
  6.5 30.9 %copy-start.4 = (s32[1536]{0:T(1024)S(1)}, s32[1536]{0:T(1024)}, u32[]{:S(2)}) copy-start(s32[1536]{0:T(1024)} %param.19) | copy-start | bytes 18436
  6.5 74.8 %all-gather.3.cloned.1.call-start = ((), (), s32[]{:S(2)}) async-start(), calls=%async_computation | async-start | bytes 1671168 | tf_op jit(solution)/shard_map/all_gather | solution.py:86
  9.8 45.9 %copy-start.3 = (bf16[2,64,1536]{2,1,0:T(8,128)(2,1)}, bf16[2,64,1536]{2,1,0:T(8,128)(2,1)S(1)}, u32[]{:S(2)}) copy-start(bf16[2,64,1536]{2,1,0:T(8,128)(2,1)S(1)} %fusion.27) | copy-start | bytes 1179652
  12.3 1.6 %collective-permute-start = (bf16[64,1536]{1,0:T(8,128)(2,1)S(1)}, bf16[64,1536]{1,0:T(8,128)(2,1)S(1)}, u32[]{:S(2)}, u32[]{:S(2)}) collective-permute-start(bf16[64,1536]{1,0:T(8,128)(2,1)S(1)} %get-tuple-element.6), channel_id=1, source_target_pairs={{0,1},{1,0},{2,3},{3,2},{4,5},{5,4},{6,7},{7,6},{8,9},{9,8},{10,11... | collective-permute-start | bytes 589832 | tf_op jit(solution)/shard_map/ppermute | solution.py:11
  13.9 23.5 %collective-permute-start.1 = (bf16[64,1536]{1,0:T(8,128)(2,1)S(1)}, bf16[64,1536]{1,0:T(8,128)(2,1)S(1)}, u32[]{:S(2)}, u32[]{:S(2)}) collective-permute-start(bf16[64,1536]{1,0:T(8,128)(2,1)S(1)} %collective-permute-done), channel_id=1, source_target_pairs={{0,2},{1,3},{2,0},{3,1},{4,6},{5,7},{6,4},{7,5},{8,10},{9,11},{10,... | collective-permute-start | bytes 589832 | tf_op jit(solution)/shard_map/ppermute | solution.py:11
  37.4 11.5 %collective-permute-start.2 = (bf16[64,1536]{1,0:T(8,128)(2,1)S(1)}, bf16[64,1536]{1,0:T(8,128)(2,1)}, u32[]{:S(2)}, u32[]{:S(2)}) collective-permute-start(bf16[64,1536]{1,0:T(8,128)(2,1)S(1)} %collective-permute-done.1), channel_id=1, source_target_pairs={{0,4},{1,5},{2,6},{3,7},{4,0},{5,1},{6,2},{7,3},{8,12},{9,13},{10,... | collective-permute-start | bytes 589832 | tf_op jit(solution)/shard_map/ppermute | solution.py:11
  48.9 28.7 %collective-permute-start.3 = (bf16[64,1536]{1,0:T(8,128)(2,1)}, bf16[64,1536]{1,0:T(8,128)(2,1)S(1)}, u32[]{:S(2)}, u32[]{:S(2)}) collective-permute-start(bf16[64,1536]{1,0:T(8,128)(2,1)} %collective-permute-done.2), channel_id=1, source_target_pairs={{0,8},{1,9},{2,10},{3,11},{4,12},{5,13},{6,14},{7,15},{8,0},{9,1},... | collective-permute-start | bytes 589832 | tf_op jit(solution)/shard_map/ppermute | solution.py:11
  48.9 6.8 %copy-start.5 = (bf16[1536]{0:T(1024)(128)(2,1)S(1)}, bf16[1536]{0:T(1024)(128)(2,1)}, u32[]{:S(2)}) copy-start(bf16[1536]{0:T(1024)(128)(2,1)} %param.16) | copy-start | bytes 9220
  55.8 13.4 %copy-start.1 = (f32[1536]{0:T(1024)S(1)}, f32[1536]{0:T(1024)}, u32[]{:S(2)}) copy-start(f32[1536]{0:T(1024)} %param.18) | copy-start | bytes 18436
  69.2 9.0 %slice-start = ((bf16[2,64,1536]{2,1,0:T(8,128)(2,1)}), bf16[1,64,1536]{2,1,0:T(8,128)(2,1)S(1)}, s32[]{:S(2)}) async-start(bf16[2,64,1536]{2,1,0:T(8,128)(2,1)} %copy-done.3), calls=%async_computation.1 | async-start | bytes 393216 | tf_op jit(solution)/shard_map/slice | solution.py:71
  81.3 2.7 %copy-start.6 = (bf16[2,1024,384]{2,1,0:T(8,128)(2,1)S(1)}, bf16[2,1024,384]{2,1,0:T(8,128)(2,1)}, u32[]{:S(2)}) copy-start(bf16[2,1024,384]{2,1,0:T(8,128)(2,1)} %all-gather.3.cloned.1.call-done) | copy-start | bytes 4718596
Sparse Core Ops, SparseCore 0:
  12.3 45.7 all-gather.2
where the time goes:
time: 102 us; the launch traced here: 101 us
  local copies, waits for them, and re-layouts  30.3 us (30%)
  blocking collectives  20.7 us (20%)
  matrix products  16.5 us (16%)
  between operations  13.6 us (13%)
  waiting for transfers between devices  12.6 us (12%)
  other arithmetic  4.27 us (4%)
  starting transfers between devices  3.44 us (3%)
    all_gather x1, blocking collectives, per_device(): lax.all_gather(usable_flag, 'tok', axis=1, tiled=True)  20.7 us
    gather x1, local copies, waits for them, and re-layouts, per_device(): head_weight[:, track_perm]  13.4 us
    ppermute x4, waiting for transfers between devices, swapped(): return lax.ppermute(value, axis, pairs)  12.5 us
    gather x1, local copies, waits for them, and re-layouts, per_device(): head_bias[track_perm]  8.38 us
    unnamed x17, local copies, waits for them, and re-layouts  6.77 us
    dot_general x1, matrix products, per_device(): jnp.dot(normed_out[1], head_weight[:, track_perm], preferred_element_type...  4.69 us
    dot_general x1, matrix products, per_device(): jnp.dot(normed_out[0], head_weight, preferred_element_type=jnp.float32)  3.42 us
    ppermute x4, starting transfers between devices, swapped(): return lax.ppermute(value, axis, pairs)  3.41 us
  transfers between devices with their start and end apart: 5, of which 2 were waited for; matrix products, arithmetic and copies ran while one was open for 32% of the time, Pallas kernels for 0%

commit v1 on v0

--- a/solution.py
+++ b/solution.py
@@ -3,6 +3,28 @@
 import jax.numpy as jnp
 from jax import lax
 from jax.sharding import PartitionSpec as P
+
+
+def joined_along(blocks, dim):
+    dims = list(blocks.shape[1:])
+    dims[dim] *= blocks.shape[0]
+    return jnp.moveaxis(blocks, 0, dim).reshape(dims)
+
+
+def doubled(x, axis):
+    peers = lax.axis_size(axis)
+    blocks = x[None]
+    for level in range(peers.bit_length() - 1):
+        distance = 1 << level
+        received = lax.ppermute(blocks, axis, [(i, i ^ distance) for i in range(peers)])
+        both = jnp.stack([blocks, received])
+        upper = lax.axis_index(axis) >> level & 1
+        blocks = jnp.where(upper == 0, both, both[::-1]).reshape(-1, *x.shape)
+    return blocks
+
+
+def collect(shard, axis, dim):
+    return joined_along(doubled(shard, axis), dim)
 
 
 def swapped(value, axis, distance):
@@ -84,7 +106,7 @@
         start_state,
         queries,
         lax.all_gather(key_value, "tok", axis=1, tiled=True),
-        lax.all_gather(usable_flag, "tok", axis=1, tiled=True),
+        collect(usable_flag, "tok", 1),
     )
     maxima, totals, accumulated = softmax_state
     attended = (

time: 102 us -> 92.8 us (0.910)
  blocking collectives: 20.7 us -> 0 us
  starting transfers between devices: 3.44 us -> 14.1 us
  other arithmetic: 4.27 us -> 6.19 us
    all_gather x1 -> x0, blocking collectives: 20.7 us -> none  [per_device(): lax.all_gather(usable_flag, 'tok', axis=1, tiled=True)]
    ppermute x0 -> x4, starting transfers between devices: none -> 7.76 us  [doubled(): lax.ppermute(blocks, axis, [(i, i ^ distance) for i in range(peers)])]
    ppermute x4, waiting for transfers between devices: 12.5 us -> 8.42 us  [swapped(): return lax.ppermute(value, axis, pairs)]
    ppermute x0 -> x4, waiting for transfers between devices: none -> 3.14 us  [doubled(): lax.ppermute(blocks, axis, [(i, i ^ distance) for i in range(peers)])]
    ppermute x4, starting transfers between devices: 3.41 us -> 6.32 us  [swapped(): return lax.ppermute(value, axis, pairs)]
    another operation x0 -> x6, other arithmetic: none -> 2.07 us  [doubled(): both = jnp.stack([blocks, received])]
    unnamed x17 -> x15, local copies, waits for them, and re-layouts: 6.77 us -> 6.78 us
  transfers between devices with their start and end apart: 5 -> 9, of which waited for: 2 -> 4; matrix products, arithmetic and copies ran while one was open for 32% -> 42% of each run, Pallas kernels for 0% -> 0%
where the time goes in v1:
time: 92.8 us; the launch traced here: 92.2 us
  local copies, waits for them, and re-layouts  30.3 us (33%)
  matrix products  16.5 us (18%)
  starting transfers between devices  14.1 us (15%)
  between operations  13.6 us (15%)
  waiting for transfers between devices  11.6 us (12%)
  other arithmetic  6.19 us (7%)
    gather x1, local copies, waits for them, and re-layouts, per_device(): head_weight[:, track_perm]  13.3 us
    ppermute x4, waiting for transfers between devices, swapped(): return lax.ppermute(value, axis, pairs)  8.42 us
    gather x1, local copies, waits for them, and re-layouts, per_device(): head_bias[track_perm]  8.38 us
    ppermute x4, starting transfers between devices, doubled(): lax.ppermute(blocks, axis, [(i, i ^ distance) for i in range(peers)])  7.76 us
    unnamed x15, local copies, waits for them, and re-layouts  6.78 us
    ppermute x4, starting transfers between devices, swapped(): return lax.ppermute(value, axis, pairs)  6.32 us
    dot_general x1, matrix products, per_device(): jnp.dot(normed_out[1], head_weight[:, track_perm], preferred_element_type...  4.69 us
    dot_general x1, matrix products, per_device(): jnp.dot(normed_out[0], head_weight, preferred_element_type=jnp.float32)  3.42 us
  transfers between devices with their start and end apart: 9, of which 4 were waited for; matrix products, arithmetic and copies ran while one was open for 42% of the time, Pallas kernels for 0%

profile of v1, /device:TPU:0, one launch (start us, length us, event | category | flops | bytes accessed | tf_op | source)
XLA Modules:
  0.0 92.2 jit_solution(10134519444621234286)
XLA Ops:
  6.5 0.0 copy-start
  6.5 0.0 all-gather.2.cloned.1.call-start
  6.5 0.8 fusion.39
  7.4 0.5 collective-permute-start.4
  7.9 0.7 convert_element_type.55
  8.6 1.2 %fusion.25 = f32[2,64]{1,0:T(2,128)S(1)} fusion(bf16[2,64,1536]{2,1,0:T(8,128)(2,1)} %param.10), kind=kLoop, calls=%fused_computation.31 | loop fusion | flops 589696 | bytes 393728 | tf_op jit(solution)/shard_map/reduce_sum | solution.py:40
  9.7 1.2 %fusion.27 = bf16[2,64,1536]{2,1,0:T(8,128)(2,1)S(1)} fusion(bf16[2,64,1536]{2,1,0:T(8,128)(2,1)} %param.10, f32[1536]{0:T(1024)S(1)} %convert_element_type.55, f32[2,64]{1,0:T(2,128)S(1)} %add_rsqrt_fusion.1), kind=kLoop, calls=%fused_computation.33 | loop fusion | flops 786432 | bytes 793088 | tf_op jit(solution)/shard_map/convert_element_type | solution.py:84
  10.9 0.0 copy-start.3
  10.9 2.4 %fusion.13 = bf16[2,64,384]{2,1,0:T(8,128)(2,1)} fusion(bf16[2,64,1536]{2,1,0:T(8,128)(2,1)S(1)} %fusion.27, bf16[1536,384]{1,0:T(8,128)(2,1)} %param.14), kind=kOutput, calls=%fused_computation.20 | convolution fusion | flops 151044096 | bytes 1671168 | tf_op jit(solution)/shard_map/std,de->ste/dot_general | solution.py:85
  13.3 0.0 all-gather.2.cloned.1.call-update
  13.4 0.0 collective-permute-done.4
  13.4 0.6 fusion.45
  13.9 2.5 %collective-permute-start.5 = (bf16[2,2,64]{2,1,0:T(2,128)(2,1)}, bf16[2,2,64]{2,1,0:T(2,128)(2,1)}, u32[]{:S(2)}, u32[]{:S(2)}) collective-permute-start(bf16[2,2,64]{2,1,0:T(2,128)(2,1)} %get-tuple-element.8), channel_id=1, source_target_pairs={{0,2},{1,3},{2,0},{3,1},{4,6},{5,7},{6,4},{7,5},{8,10},{9,11},{10,... | collective-permute-start | bytes 1544 | tf_op jit(solution)/shard_map/ppermute | solution.py:19
  16.5 0.0 copy-done.2
  16.5 0.3 collective-permute-start
  16.8 1.6 %collective-permute-done.5 = bf16[2,2,64]{2,1,0:T(2,128)(2,1)} collective-permute-done((bf16[2,2,64]{2,1,0:T(2,128)(2,1)}, bf16[2,2,64]{2,1,0:T(2,128)(2,1)}, u32[]{:S(2)}, u32[]{:S(2)}) %collective-permute-start.5) | collective-permute-done | bytes 544 | tf_op jit(solution)/shard_map/ppermute | solution.py:19
  18.3 0.6 pad_maximum_fusion.3
  19.0 2.2 %collective-permute-start.6 = (bf16[4,2,64]{2,1,0:T(2,128)(2,1)S(1)}, bf16[4,2,64]{2,1,0:T(2,128)(2,1)S(1)}, u32[]{:S(2)}, u32[]{:S(2)}) collective-permute-start(bf16[4,2,64]{2,1,0:T(2,128)(2,1)S(1)} %bitcast.57), channel_id=1, source_target_pairs={{0,4},{1,5},{2,6},{3,7},{4,0},{5,1},{6,2},{7,3},{8,12},{9,13},{10,... | collective-permute-start | bytes 3080 | tf_op jit(solution)/shard_map/ppermute | solution.py:19
  21.2 1.6 %collective-permute-done.6 = bf16[4,2,64]{2,1,0:T(2,128)(2,1)S(1)} collective-permute-done((bf16[4,2,64]{2,1,0:T(2,128)(2,1)S(1)}, bf16[4,2,64]{2,1,0:T(2,128)(2,1)S(1)}, u32[]{:S(2)}, u32[]{:S(2)}) %collective-permute-start.6) | collective-permute-done | bytes 1056 | tf_op jit(solution)/shard_map/ppermute | solution.py:19
  22.7 0.0 collective-permute-done
  22.7 2.0 %collective-permute-start.1 = (bf16[64,1536]{1,0:T(8,128)(2,1)S(1)}, bf16[64,1536]{1,0:T(8,128)(2,1)S(1)}, u32[]{:S(2)}, u32[]{:S(2)}) collective-permute-start(bf16[64,1536]{1,0:T(8,128)(2,1)S(1)} %collective-permute-done), channel_id=1, source_target_pairs={{0,2},{1,3},{2,0},{3,1},{4,6},{5,7},{6,4},{7,5},{8,10},{9,11},{10,... | collective-permute-start | bytes 589832 | tf_op jit(solution)/shard_map/ppermute | solution.py:33
  24.7 2.6 %collective-permute-start.7 = (bf16[8,2,64]{2,1,0:T(2,128)(2,1)S(1)}, bf16[8,2,64]{2,1,0:T(2,128)(2,1)S(1)}, u32[]{:S(2)}, u32[]{:S(2)}) collective-permute-start(bf16[8,2,64]{2,1,0:T(2,128)(2,1)S(1)} %bitcast.55), channel_id=1, source_target_pairs={{0,8},{1,9},{2,10},{3,11},{4,12},{5,13},{6,14},{7,15},{8,0},{9,1},... | collective-permute-start | bytes 6152 | tf_op jit(solution)/shard_map/ppermute | solution.py:19
  27.3 2.2 %collective-permute-done.1 = bf16[64,1536]{1,0:T(8,128)(2,1)S(1)} collective-permute-done((bf16[64,1536]{1,0:T(8,128)(2,1)S(1)}, bf16[64,1536]{1,0:T(8,128)(2,1)S(1)}, u32[]{:S(2)}, u32[]{:S(2)}) %collective-permute-start.1) | collective-permute-done | bytes 196640 | tf_op jit(solution)/shard_map/ppermute | solution.py:33
  29.5 1.6 %collective-permute-start.2 = (bf16[64,1536]{1,0:T(8,128)(2,1)S(1)}, bf16[64,1536]{1,0:T(8,128)(2,1)}, u32[]{:S(2)}, u32[]{:S(2)}) collective-permute-start(bf16[64,1536]{1,0:T(8,128)(2,1)S(1)} %collective-permute-done.1), channel_id=1, source_target_pairs={{0,4},{1,5},{2,6},{3,7},{4,0},{5,1},{6,2},{7,3},{8,12},{9,13},{10,... | collective-permute-start | bytes 589832 | tf_op jit(solution)/shard_map/ppermute | solution.py:33
  31.1 6.8 %copy.21 = bf16[1536,1536]{0,1:T(8,128)(2,1)} copy(bf16[1536,1536]{1,0:T(8,128)(2,1)} %param.17) | data formatting | bytes 9437184 | tf_op args[7]
  37.9 0.0 copy-done.5
  37.9 0.0 copy-start.1
  37.9 13.3 %gather_fusion = bf16[1536,1536]{1,0:T(8,128)(2,1)} fusion(bf16[1536,1536]{0,1:T(8,128)(2,1)} %copy.21, s32[2048]{0:T(1024)S(1)} %pad_clamp_fusion), kind=kCustom, calls=%fused_computation | custom fusion | bytes 9443328 | tf_op jit(solution)/shard_map/gather | solution.py:125
  51.2 8.4 %gather_fusion.1 = f32[1536]{0:T(1024)S(1)} fusion(f32[1536]{0:T(1024)S(1)} %copy-done.1, s32[2048]{0:T(1024)S(1)} %pad_clamp_fusion), kind=kCustom, calls=%fused_computation.1 | custom fusion | bytes 18432 | tf_op jit(solution)/shard_map/gather | solution.py:126
  59.6 0.0 collective-permute-done.7
  59.7 0.0 collective-permute-done.2
  59.7 2.5 %collective-permute-start.3 = (bf16[64,1536]{1,0:T(8,128)(2,1)}, bf16[64,1536]{1,0:T(8,128)(2,1)S(1)}, u32[]{:S(2)}, u32[]{:S(2)}) collective-permute-start(bf16[64,1536]{1,0:T(8,128)(2,1)} %collective-permute-done.2), channel_id=1, source_target_pairs={{0,8},{1,9},{2,10},{3,11},{4,12},{5,13},{6,14},{7,15},{8,0},{9,1},... | collective-permute-start | bytes 589832 | tf_op jit(solution)/shard_map/ppermute | solution.py:33
  62.2 0.1 gt.24
  62.3 6.2 %collective-permute-done.3 = bf16[64,1536]{1,0:T(8,128)(2,1)S(1)} collective-permute-done((bf16[64,1536]{1,0:T(8,128)(2,1)}, bf16[64,1536]{1,0:T(8,128)(2,1)S(1)}, u32[]{:S(2)}, u32[]{:S(2)}) %collective-permute-start.3) | collective-permute-done | bytes 196640 | tf_op jit(solution)/shard_map/ppermute | solution.py:33
  68.5 0.3 rev.15
  68.8 0.1 fusion.28
  69.0 0.1 fusion.36
  69.1 2.2 %fusion.10 = bf16[2,64,768]{2,1,0:T(8,128)(2,1)S(1)} fusion(bf16[1536,768]{1,0:T(8,128)(2,1)} %param.13, bf16[1,64,1536]{2,1,0:T(8,128)(2,1)S(1)} %fusion.36, bf16[1,64,1536]{2,1,0:T(8,128)(2,1)S(1)} %slice-done), kind=kOutput, calls=%fused_computation.19 | convolution fusion | flops 302284800 | bytes 2949120 | tf_op jit(solution)/shard_map/std,de->ste/dot_general | solution.py:95
  71.3 1.0 %reshape.63 = bf16[2,256,192]{2,1,0:T(8,128)(2,1)} reshape(bf16[2,64,768]{2,1,0:T(8,128)(2,1)S(1)} %fusion.10) | data formatting | bytes 393216 | tf_op jit(solution)/shard_map/reshape | solution.py:98
  72.3 2.0 %fusion.4 = (f32[2,256]{1,0:T(2,128)S(1)}, f32[2,256,1024]{2,1,0:T(8,128)S(1)}) fusion(pred[2,1024]{1,0:T(4,128)(4,1)S(1)} %gt.24, bf16[2,256,192]{2,1,0:T(8,128)(2,1)} %reshape.63, bf16[2,1024,384]{2,1,0:T(8,128)(2,1)} %all-gather.2.cloned.1.call-done), kind=kOutput, calls=%fused_computation.10 | convolution fusion | flops 202898944 | bytes 3411968 | tf_op jit(solution)/shard_map/srd,skd->srk/dot_general | solution.py:50
  74.3 0.6 fusion.5
  74.9 1.2 %fusion.9 = bf16[2,256,192]{1,2,0:T(8,128)(2,1)S(1)} fusion(f32[2,256,1024]{2,1,0:T(8,128)S(1)} %get-tuple-element.12, bf16[2,1024,384]{2,1,0:T(8,128)(2,1)S(1)} %copy-done.6, f32[2,256]{1,0:T(2,128)S(1)} %broadcast_maximum_fusion, pred[2,1024]{1,0:T(4,128)(4,1)S(1)} %gt.24, f32[2,256]{1,0:T(2,128)S(1)} %fusion.5), kind=kOutput, calls=%fused_computation.18 | convolution fusion | flops 204144640 | bytes 3350528 | tf_op jit(solution)/shard_map/srk,skd->srd/dot_general | solution.py:58
  76.1 0.1 copy.20
  76.3 0.3 reshape.64
  76.5 0.6 multiply_reduce_fusion
  77.1 0.2 multiply_convert_fusion
  77.3 3.4 %fusion.31 = bf16[64,1536]{1,0:T(8,128)(2,1)S(1)} fusion(bf16[1536,1536]{1,0:T(8,128)(2,1)} %param.17, bf16[2,64,1536]{2,1,0:T(8,128)(2,1)S(1)} %multiply_convert_fusion, f32[1536]{0:T(1024)S(1)} %copy-done.1), kind=kOutput, calls=%fused_computation.42 | convolution fusion | flops 302776320 | bytes 5120000 | tf_op jit(solution)/shard_map/dot_general | solution.py:122
  80.7 4.7 %add_multiply_fusion = f32[64,1536]{1,0:T(8,128)} fusion(bf16[1536,1536]{1,0:T(8,128)(2,1)} %gather_fusion, bf16[64,1536]{1,0:T(8,128)(2,1)S(1)} %fusion.31, bf16[2,64,1536]{2,1,0:T(8,128)(2,1)S(1)} %multiply_convert_fusion, f32[1536]{0:T(1024)S(1)} %gather_fusion.1), kind=kOutput, calls=%fused_computation.48 | convolution fusion | flops 303169536 | bytes 5513216 | tf_op jit(solution)/shard_map/dot_general | solution.py:125
  (27 shorter events, 0.2 us)
Async XLA Ops:
  6.5 70.0 %copy-start = (bf16[768,1536]{1,0:T(8,128)(2,1)S(1)}, bf16[768,1536]{1,0:T(8,128)(2,1)}, u32[]{:S(2)}) copy-start(bf16[768,1536]{1,0:T(8,128)(2,1)} %param.15) | copy-start | bytes 7077892
  6.5 9.9 %copy-start.2 = (bf16[2,64,1536]{2,1,0:T(8,128)(2,1)S(1)}, bf16[2,64,1536]{2,1,0:T(8,128)(2,1)}, u32[]{:S(2)}) copy-start(bf16[2,64,1536]{2,1,0:T(8,128)(2,1)} %param.10) | copy-start | bytes 1179652
  6.5 14.6 %copy-start.4 = (s32[1536]{0:T(1024)S(1)}, s32[1536]{0:T(1024)}, u32[]{:S(2)}) copy-start(s32[1536]{0:T(1024)} %param.19) | copy-start | bytes 18436
  6.5 65.7 %all-gather.2.cloned.1.call-start = ((), (), s32[]{:S(2)}) async-start(), calls=%async_computation | async-start | bytes 1671168 | tf_op jit(solution)/shard_map/all_gather | solution.py:108
  7.4 6.0 %collective-permute-start.4 = (bf16[1,2,64]{2,1,0:T(2,128)(2,1)S(1)}, bf16[1,2,64]{2,1,0:T(2,128)(2,1)S(1)}, u32[]{:S(2)}, u32[]{:S(2)}) collective-permute-start(bf16[1,2,64]{2,1,0:T(2,128)(2,1)S(1)} %get-tuple-element.10), channel_id=1, source_target_pairs={{0,1},{1,0},{2,3},{3,2},{4,5},{5,4},{6,7},{7,6},{8,9},{9,8},{10,11... | collective-permute-start | bytes 776 | tf_op jit(solution)/shard_map/ppermute | solution.py:19
  10.9 27.0 %copy-start.3 = (bf16[2,64,1536]{2,1,0:T(8,128)(2,1)}, bf16[2,64,1536]{2,1,0:T(8,128)(2,1)S(1)}, u32[]{:S(2)}) copy-start(bf16[2,64,1536]{2,1,0:T(8,128)(2,1)S(1)} %fusion.27) | copy-start | bytes 1179652
  13.9 4.4 %collective-permute-start.5 = (bf16[2,2,64]{2,1,0:T(2,128)(2,1)}, bf16[2,2,64]{2,1,0:T(2,128)(2,1)}, u32[]{:S(2)}, u32[]{:S(2)}) collective-permute-start(bf16[2,2,64]{2,1,0:T(2,128)(2,1)} %get-tuple-element.8), channel_id=1, source_target_pairs={{0,2},{1,3},{2,0},{3,1},{4,6},{5,7},{6,4},{7,5},{8,10},{9,11},{10,... | collective-permute-start | bytes 1544 | tf_op jit(solution)/shard_map/ppermute | solution.py:19
  16.5 6.2 %collective-permute-start = (bf16[64,1536]{1,0:T(8,128)(2,1)S(1)}, bf16[64,1536]{1,0:T(8,128)(2,1)S(1)}, u32[]{:S(2)}, u32[]{:S(2)}) collective-permute-start(bf16[64,1536]{1,0:T(8,128)(2,1)S(1)} %get-tuple-element.6), channel_id=1, source_target_pairs={{0,1},{1,0},{2,3},{3,2},{4,5},{5,4},{6,7},{7,6},{8,9},{9,8},{10,11... | collective-permute-start | bytes 589832 | tf_op jit(solution)/shard_map/ppermute | solution.py:33
  19.0 3.7 %collective-permute-start.6 = (bf16[4,2,64]{2,1,0:T(2,128)(2,1)S(1)}, bf16[4,2,64]{2,1,0:T(2,128)(2,1)S(1)}, u32[]{:S(2)}, u32[]{:S(2)}) collective-permute-start(bf16[4,2,64]{2,1,0:T(2,128)(2,1)S(1)} %bitcast.57), channel_id=1, source_target_pairs={{0,4},{1,5},{2,6},{3,7},{4,0},{5,1},{6,2},{7,3},{8,12},{9,13},{10,... | collective-permute-start | bytes 3080 | tf_op jit(solution)/shard_map/ppermute | solution.py:19
  22.7 6.8 %collective-permute-start.1 = (bf16[64,1536]{1,0:T(8,128)(2,1)S(1)}, bf16[64,1536]{1,0:T(8,128)(2,1)S(1)}, u32[]{:S(2)}, u32[]{:S(2)}) collective-permute-start(bf16[64,1536]{1,0:T(8,128)(2,1)S(1)} %collective-permute-done), channel_id=1, source_target_pairs={{0,2},{1,3},{2,0},{3,1},{4,6},{5,7},{6,4},{7,5},{8,10},{9,11},{10,... | collective-permute-start | bytes 589832 | tf_op jit(solution)/shard_map/ppermute | solution.py:33
  24.7 34.9 %collective-permute-start.7 = (bf16[8,2,64]{2,1,0:T(2,128)(2,1)S(1)}, bf16[8,2,64]{2,1,0:T(2,128)(2,1)S(1)}, u32[]{:S(2)}, u32[]{:S(2)}) collective-permute-start(bf16[8,2,64]{2,1,0:T(2,128)(2,1)S(1)} %bitcast.55), channel_id=1, source_target_pairs={{0,8},{1,9},{2,10},{3,11},{4,12},{5,13},{6,14},{7,15},{8,0},{9,1},... | collective-permute-start | bytes 6152 | tf_op jit(solution)/shard_map/ppermute | solution.py:19
  29.5 30.1 %collective-permute-start.2 = (bf16[64,1536]{1,0:T(8,128)(2,1)S(1)}, bf16[64,1536]{1,0:T(8,128)(2,1)}, u32[]{:S(2)}, u32[]{:S(2)}) collective-permute-start(bf16[64,1536]{1,0:T(8,128)(2,1)S(1)} %collective-permute-done.1), channel_id=1, source_target_pairs={{0,4},{1,5},{2,6},{3,7},{4,0},{5,1},{6,2},{7,3},{8,12},{9,13},{10,... | collective-permute-start | bytes 589832 | tf_op jit(solution)/shard_map/ppermute | solution.py:33
  31.1 6.8 %copy-start.5 = (bf16[1536]{0:T(1024)(128)(2,1)S(1)}, bf16[1536]{0:T(1024)(128)(2,1)}, u32[]{:S(2)}) copy-start(bf16[1536]{0:T(1024)(128)(2,1)} %param.16) | copy-start | bytes 9220
  37.9 13.3 %copy-start.1 = (f32[1536]{0:T(1024)S(1)}, f32[1536]{0:T(1024)}, u32[]{:S(2)}) copy-start(f32[1536]{0:T(1024)} %param.18) | copy-start | bytes 18436
  51.2 17.9 %slice-start = ((bf16[2,64,1536]{2,1,0:T(8,128)(2,1)}), bf16[1,64,1536]{2,1,0:T(8,128)(2,1)S(1)}, s32[]{:S(2)}) async-start(bf16[2,64,1536]{2,1,0:T(8,128)(2,1)} %copy-done.3), calls=%async_computation.1 | async-start | bytes 393216 | tf_op jit(solution)/shard_map/slice | solution.py:93
  59.7 8.8 %collective-permute-start.3 = (bf16[64,1536]{1,0:T(8,128)(2,1)}, bf16[64,1536]{1,0:T(8,128)(2,1)S(1)}, u32[]{:S(2)}, u32[]{:S(2)}) collective-permute-start(bf16[64,1536]{1,0:T(8,128)(2,1)} %collective-permute-done.2), channel_id=1, source_target_pairs={{0,8},{1,9},{2,10},{3,11},{4,12},{5,13},{6,14},{7,15},{8,0},{9,1},... | collective-permute-start | bytes 589832 | tf_op jit(solution)/shard_map/ppermute | solution.py:33
  72.3 2.7 %copy-start.6 = (bf16[2,1024,384]{2,1,0:T(8,128)(2,1)S(1)}, bf16[2,1024,384]{2,1,0:T(8,128)(2,1)}, u32[]{:S(2)}) copy-start(bf16[2,1024,384]{2,1,0:T(8,128)(2,1)} %all-gather.2.cloned.1.call-done) | copy-start | bytes 4718596
Sparse Core Ops, SparseCore 0:
  13.5 42.6 all-gather.1
